TPU v7x, 32 devices: a whole 2x2x4 slice. The times are simulated.
32 devices in a mesh: dp: 16 (over z, y, core), tensor: 2 (over x).
Axes of the slice: x: 2, y: 2, z: 4, core: 2. Of those that a mesh axis runs over, the one named last changes fastest.
Arguments:
- patches: bfloat16 [50176, 768], P(('dp', 'tensor')), may hold values from -6 to 6
- visible: int32 [1024, 49], P(('dp', 'tensor')), may hold values from 0 to 195, as said below
- pos_table: float32 [196, 768], replicated, may hold values from -6 to 6
- cotangent: bfloat16 [50176, 768], P(('dp', 'tensor')), may hold values from -6 to 6
- step_count: int32 [1], replicated, may hold values from 2 to 20
- w_qkv: float32 [768, 3, 768], P('dp', None, 'tensor'), may hold values from -0.21875 to 0.21875
- m_qkv: float32 [768, 3, 768], P('dp', None, 'tensor'), may hold values from -0.00018793954 to 0.00018793954
- v_qkv: float32 [768, 3, 768], P('dp', None, 'tensor'), may hold values from 7.48811e-09 to 2.9669868e-08
- w_proj: float32 [768, 768], P('tensor', 'dp'), may hold values from -0.875 to 0.875
- m_proj: float32 [768, 768], P('tensor', 'dp'), may hold values from -0.00018793954 to 0.00018793954
- v_proj: float32 [768, 768], P('tensor', 'dp'), may hold values from 7.48811e-09 to 2.9669868e-08
- w_fc1: float32 [768, 4, 768], P('dp', None, 'tensor'), may hold values from -0.21875 to 0.21875
- m_fc1: float32 [768, 4, 768], P('dp', None, 'tensor'), may hold values from -0.00018793954 to 0.00018793954
- v_fc1: float32 [768, 4, 768], P('dp', None, 'tensor'), may hold values from 7.48811e-09 to 2.9669868e-08
- w_fc2: float32 [4, 768, 768], P(None, 'tensor', 'dp'), may hold values from -0.109375 to 0.109375
- m_fc2: float32 [4, 768, 768], P(None, 'tensor', 'dp'), may hold values from -0.00018793954 to 0.00018793954
- v_fc2: float32 [4, 768, 768], P(None, 'tensor', 'dp'), may hold values from 7.48811e-09 to 2.9669868e-08
- split_bias: float32 [6, 768], P(None, 'tensor'), may hold values from -3 to 3
- m_split: float32 [6, 768], P(None, 'tensor'), may hold values from -0.0005638186 to 0.0005638186
- v_split: float32 [6, 768], P(None, 'tensor'), may hold values from 6.640399e-08 to 2.6844165e-07
- norm_bias: float32 [6, 768], replicated, may hold values from -1.2 to 1.8
- m_norm: float32 [6, 768], replicated, may hold values from -0.0005638186 to 0.0005638186
- v_norm: float32 [6, 768], replicated, may hold values from 6.640399e-08 to 2.6844165e-07
Outputs:
- block_out: bfloat16 [50176, 768], P(('dp', 'tensor'))
- input_grad: float32 [50176, 768], P(('dp', 'tensor'))
- grad_norm: float32 [], replicated
- new_qkv: float32 [768, 3, 768], P('dp', None, 'tensor')
- first_qkv: float32 [768, 3, 768], P('dp', None, 'tensor')
- second_qkv: float32 [768, 3, 768], P('dp', None, 'tensor')
- new_proj: float32 [768, 768], P('tensor', 'dp')
- first_proj: float32 [768, 768], P('tensor', 'dp')
- second_proj: float32 [768, 768], P('tensor', 'dp')
- new_fc1: float32 [768, 4, 768], P('dp', None, 'tensor')
- first_fc1: float32 [768, 4, 768], P('dp', None, 'tensor')
- second_fc1: float32 [768, 4, 768], P('dp', None, 'tensor')
- new_fc2: float32 [4, 768, 768], P(None, 'tensor', 'dp')
- first_fc2: float32 [4, 768, 768], P(None, 'tensor', 'dp')
- second_fc2: float32 [4, 768, 768], P(None, 'tensor', 'dp')
- new_split: float32 [6, 768], P(None, 'tensor')
- first_split: float32 [6, 768], P(None, 'tensor')
- second_split: float32 [6, 768], P(None, 'tensor')
- new_norm: float32 [6, 768], replicated
- first_norm: float32 [6, 768], replicated
- second_norm: float32 [6, 768], replicated
Inputs may be any that keep to these rules, and one draw needn't show every extreme that they name: `visible`: the 49 entries of an image are distinct patch positions.
All inputs are finite; a program needn't handle non-finite values.
Results may differ from a plain program's by a relative error of at most 0.014.
Values may be sent and summed in bfloat16 or wider, within the bound.
No kernel may reach another device: no remote copies, remote signals or barrier semaphores. Data moves between devices by JAX's collectives and lax.ppermute only.
A program may use at most 256 MiB of HBM per device.

v0:
```python
import jax
import jax.numpy as jnp
from jax import lax
from jax.sharding import PartitionSpec as P

HD = 64
VISIBLE = 49
norm_eps = 1e-06
beta_one = 0.9
beta_two = 0.95
adam_eps = 1e-08
clip_value = 1.0
matrix_rate = 0.02
proj_rate = 0.08
vector_rate = 0.2
matrix_decay = 0.05


def layer_norm(values, row_gain, row_shift):
    row_mean = jnp.mean(values, axis=-1, keepdims=True)
    centred = values - row_mean
    variance = jnp.mean(centred * centred, axis=-1, keepdims=True)
    return centred * lax.rsqrt(variance + norm_eps) * row_gain + row_shift


def adam_update(
    weight, gradient, first_moment, second, factor, bias_first, bias_second, learn_rate, decay_rate
):
    clipped = gradient * factor
    first_new = beta_one * first_moment + (1.0 - beta_one) * clipped
    second_new = beta_two * second + (1.0 - beta_two) * clipped * clipped
    direction = first_new / bias_first / (jnp.sqrt(second_new / bias_second) + adam_eps)
    return (weight - learn_rate * (direction + decay_rate * weight), first_new, second_new)


def transpose_dot(left_side, right_side):
    return lax.dot_general(
        left_side, right_side, (((0,), (0,)), ((), ())), preferred_element_type=jnp.float32
    )


def dot_back(left_side, right_side):
    return lax.dot_general(
        left_side, right_side, (((1,), (1,)), ((), ())), preferred_element_type=jnp.float32
    )


def square_sum(arrays):
    total = jnp.sum(arrays[0] * arrays[0])
    for member in arrays[1:]:
        total = total + jnp.sum(member * member)
    return total


def standard_normal(values):
    cumulative = 0.5 + 0.5 * lax.erf(values * 0.5**0.5)
    density = jnp.exp(-0.5 * values * values) * (0.5 / jnp.pi) ** 0.5
    return (cumulative, density)


def body(
    patches,
    visible,
    pos_table,
    cotangent,
    step_count,
    w_qkv,
    m_qkv,
    v_qkv,
    w_proj,
    m_proj,
    v_proj,
    w_fc1,
    m_fc1,
    v_fc1,
    w_fc2,
    m_fc2,
    v_fc2,
    split_bias,
    m_split,
    v_split,
    norm_bias,
    m_norm,
    v_norm,
):
    model_width = patches.shape[1]
    shard_rows = w_qkv.shape[0]
    shard_width = w_qkv.shape[2]
    halves = model_width // shard_width
    attn_scale = HD ** (-0.5)
    full_rows = patches.shape[0]
    every = ("tensor", "dp")
    low_type = jnp.bfloat16

    def rows_of(proj_like):
        return jnp.swapaxes(proj_like, -1, -2)

    def gather(block):
        whole = lax.all_gather(block.astype(low_type), every, axis=0, tiled=True)
        return whole.reshape(halves, model_width, block.shape[1])

    fc2_rows = jnp.transpose(w_fc2, (2, 0, 1)).reshape(shard_rows, 4 * shard_width)
    qkv_low = gather(w_qkv.reshape(shard_rows, 3 * shard_width))
    rest_low = gather(
        jnp.concatenate(
            [rows_of(w_proj), w_fc1.reshape(shard_rows, 4 * shard_width), fc2_rows], axis=1
        )
    )
    proj_low = [rest_low[t, :, :shard_width] for t in range(halves)]
    fc1_low = [rest_low[t, :, shard_width : 5 * shard_width] for t in range(halves)]
    fc2_low = [rest_low[t, :, 5 * shard_width :] for t in range(halves)]
    split_whole_bias = lax.all_gather(split_bias, "tensor", axis=0, tiled=False)
    inputs = patches.astype(jnp.float32) + jnp.take(pos_table, visible.reshape(-1), axis=0)
    normed, norm_back = jax.vjp(layer_norm, inputs, norm_bias[0], norm_bias[1])
    normed_low = normed.astype(low_type)
    heads_here = shard_width // HD
    head_shape = (full_rows // VISIBLE, VISIBLE, heads_here, HD)
    attended = jnp.zeros((full_rows, model_width), jnp.float32)
    kept = []
    for t in range(halves):
        projected = jnp.dot(normed_low, qkv_low[t], preferred_element_type=jnp.float32)
        bias_t = split_whole_bias[t]
        query_heads = (projected[:, :shard_width] + bias_t[0]).astype(low_type).reshape(head_shape)
        key_heads = projected[:, shard_width : 2 * shard_width].astype(low_type).reshape(head_shape)
        value_heads = (
            (projected[:, 2 * shard_width :] + bias_t[1]).astype(low_type).reshape(head_shape)
        )
        scores = (
            jnp.einsum(
                "bqhd,bkhd->bhqk", query_heads, key_heads, preferred_element_type=jnp.float32
            )
            * attn_scale
        )
        attention = jax.nn.softmax(scores, axis=-1)
        soft_low = attention.astype(low_type)
        mixed_low = (
            jnp.einsum("bhqk,bkhd->bqhd", soft_low, value_heads, preferred_element_type=jnp.float32)
            .reshape(full_rows, shard_width)
            .astype(low_type)
        )
        attended = attended + dot_back(mixed_low, proj_low[t])
        kept.append((query_heads, key_heads, value_heads, attention, soft_low, mixed_low))
    hidden_res = inputs + (attended + norm_bias[2])
    normed_two, norm_two_back = jax.vjp(layer_norm, hidden_res, norm_bias[3], norm_bias[4])
    normed_two_low = normed_two.astype(low_type)
    ffn_out = jnp.zeros((full_rows, model_width), jnp.float32)
    grad_out = cotangent.astype(jnp.float32)
    grad_normed_two = jnp.zeros((full_rows, model_width), jnp.float32)
    grad_fc1, grad_fc2, grad_fc1_bias = ([], [], [])
    for t in range(halves):
        pre_gelu = jnp.dot(
            normed_two_low, fc1_low[t], preferred_element_type=jnp.float32
        ) + split_whole_bias[t, 2:].reshape(-1)
        cumulative, density = standard_normal(pre_gelu)
        activated_low = (pre_gelu * cumulative).astype(low_type)
        slope_low = (cumulative + pre_gelu * density).astype(low_type)
        ffn_out = ffn_out + dot_back(activated_low, fc2_low[t])
        grad_fc2.append(transpose_dot(cotangent, activated_low).astype(low_type))
        grad_act = jnp.dot(cotangent, fc2_low[t], preferred_element_type=jnp.float32)
        grad_pre = (grad_act * slope_low.astype(jnp.float32)).astype(low_type)
        grad_fc1.append(transpose_dot(normed_two_low, grad_pre).astype(low_type))
        grad_fc1_bias.append(jnp.sum(grad_pre.astype(jnp.float32), axis=0).reshape(4, shard_width))
        grad_normed_two = grad_normed_two + dot_back(grad_pre, fc1_low[t])
    block_out = (hidden_res + (ffn_out + norm_bias[5])).astype(low_type)

    def scatter(parts):
        stacked = jnp.stack(parts).reshape(halves * model_width, parts[0].shape[1])
        return lax.psum_scatter(stacked, every, scatter_dimension=0, tiled=True).astype(jnp.float32)

    ffn_shard = scatter(
        [jnp.concatenate([grad_fc1[t], grad_fc2[t]], axis=1) for t in range(halves)]
    )
    grad_hidden_norm, grad_gain_two, grad_shift_two = norm_two_back(grad_normed_two)
    grad_hidden = grad_out + grad_hidden_norm
    grad_attn_low = grad_hidden.astype(low_type)
    grad_normed = jnp.zeros((full_rows, model_width), jnp.float32)
    grad_front, grad_query_bias = ([], [])
    for t in range(halves):
        query_heads, key_heads, value_heads, attention, soft_low, mixed_low = kept[t]
        grad_proj = transpose_dot(grad_attn_low, mixed_low).astype(low_type)
        grad_mixed = (
            jnp.dot(grad_attn_low, proj_low[t], preferred_element_type=jnp.float32)
            .astype(low_type)
            .reshape(head_shape)
        )
        grad_soft = jnp.einsum(
            "bqhd,bkhd->bhqk", grad_mixed, value_heads, preferred_element_type=jnp.float32
        )
        grad_values = jnp.einsum(
            "bhqk,bqhd->bkhd", soft_low, grad_mixed, preferred_element_type=jnp.float32
        ).astype(low_type)
        grad_scores = (
            attention * (grad_soft - jnp.sum(grad_soft * attention, axis=-1, keepdims=True))
        ).astype(low_type)
        grad_queries = (
            jnp.einsum(
                "bhqk,bkhd->bqhd", grad_scores, key_heads, preferred_element_type=jnp.float32
            )
            * attn_scale
        ).astype(low_type)
        grad_keys = (
            jnp.einsum(
                "bhqk,bqhd->bkhd", grad_scores, query_heads, preferred_element_type=jnp.float32
            )
            * attn_scale
        ).astype(low_type)
        grad_query_rows = grad_queries.reshape(full_rows, shard_width)
        grad_value_rows = grad_values.reshape(full_rows, shard_width)
        grad_proj_in = jnp.concatenate(
            [grad_query_rows, grad_keys.reshape(full_rows, shard_width), grad_value_rows], axis=1
        )
        grad_qkv = transpose_dot(normed_low, grad_proj_in).astype(low_type)
        grad_front.append(jnp.concatenate([grad_qkv, grad_proj], axis=1))
        grad_normed = grad_normed + dot_back(grad_proj_in, qkv_low[t])
        grad_query_bias.append(
            jnp.stack(
                [
                    jnp.sum(grad_query_rows.astype(jnp.float32), axis=0),
                    jnp.sum(grad_value_rows.astype(jnp.float32), axis=0),
                ]
            )
        )
    front_shard = scatter(grad_front)
    grad_input_norm, grad_gain_one, grad_shift_one = norm_back(grad_normed)
    input_grad = grad_hidden + grad_input_norm
    grad_split = jnp.stack(
        [jnp.concatenate([grad_query_bias[t], grad_fc1_bias[t]]) for t in range(halves)]
    )
    grad_norm_rows = jnp.stack(
        [
            grad_gain_one,
            grad_shift_one,
            jnp.sum(grad_attn_low.astype(jnp.float32), axis=0),
            grad_gain_two,
            grad_shift_two,
            jnp.sum(grad_out, axis=0),
        ]
    )
    shards = (
        front_shard[:, : 3 * shard_width].reshape(shard_rows, 3, shard_width),
        rows_of(front_shard[:, 3 * shard_width :]),
        ffn_shard[:, : 4 * shard_width].reshape(shard_rows, 4, shard_width),
        jnp.transpose(
            ffn_shard[:, 4 * shard_width :].reshape(shard_rows, 4, shard_width), (1, 2, 0)
        ),
    )
    local_square = square_sum((front_shard, ffn_shard))
    norm_total, split_whole, square_total = lax.psum(
        (grad_norm_rows, grad_split, local_square), ("dp", "tensor")
    )
    split_total = split_whole[lax.axis_index("tensor")]
    grad_norm = jnp.sqrt(
        square_total + jnp.sum(norm_total * norm_total) + jnp.sum(split_whole * split_whole)
    )
    factor = jnp.minimum(1.0, clip_value / (grad_norm + 1e-06))
    step_value = step_count[0].astype(jnp.float32)
    bias_first = 1.0 - jnp.power(beta_one, step_value)
    bias_second = 1.0 - jnp.power(beta_two, step_value)
    qkv_out = adam_update(
        w_qkv, shards[0], m_qkv, v_qkv, factor, bias_first, bias_second, matrix_rate, matrix_decay
    )
    proj_out = adam_update(
        w_proj, shards[1], m_proj, v_proj, factor, bias_first, bias_second, proj_rate, matrix_decay
    )
    fc1_out = adam_update(
        w_fc1, shards[2], m_fc1, v_fc1, factor, bias_first, bias_second, matrix_rate, matrix_decay
    )
    fc2_out = adam_update(
        w_fc2, shards[3], m_fc2, v_fc2, factor, bias_first, bias_second, matrix_rate, matrix_decay
    )
    split_out = adam_update(
        split_bias, split_total, m_split, v_split, factor, bias_first, bias_second, vector_rate, 0.0
    )
    norm_out = adam_update(
        norm_bias, norm_total, m_norm, v_norm, factor, bias_first, bias_second, vector_rate, 0.0
    )
    return (
        block_out,
        input_grad,
        grad_norm,
        qkv_out[0],
        qkv_out[1],
        qkv_out[2],
        proj_out[0],
        proj_out[1],
        proj_out[2],
        fc1_out[0],
        fc1_out[1],
        fc1_out[2],
        fc2_out[0],
        fc2_out[1],
        fc2_out[2],
        split_out[0],
        split_out[1],
        split_out[2],
        norm_out[0],
        norm_out[1],
        norm_out[2],
    )


def solution(mesh):
    return jax.shard_map(
        body,
        mesh=mesh,
        in_specs=(
            P(("dp", "tensor"), None),
            P(("dp", "tensor"), None),
            P(),
            P(("dp", "tensor"), None),
            P(),
            P("dp", None, "tensor"),
            P("dp", None, "tensor"),
            P("dp", None, "tensor"),
            P("tensor", "dp"),
            P("tensor", "dp"),
            P("tensor", "dp"),
            P("dp", None, "tensor"),
            P("dp", None, "tensor"),
            P("dp", None, "tensor"),
            P(None, "tensor", "dp"),
            P(None, "tensor", "dp"),
            P(None, "tensor", "dp"),
            P(None, "tensor"),
            P(None, "tensor"),
            P(None, "tensor"),
            P(),
            P(),
            P(),
        ),
        out_specs=(
            P(("dp", "tensor"), None),
            P(("dp", "tensor"), None),
            P(),
            P("dp", None, "tensor"),
            P("dp", None, "tensor"),
            P("dp", None, "tensor"),
            P("tensor", "dp"),
            P("tensor", "dp"),
            P("tensor", "dp"),
            P("dp", None, "tensor"),
            P("dp", None, "tensor"),
            P("dp", None, "tensor"),
            P(None, "tensor", "dp"),
            P(None, "tensor", "dp"),
            P(None, "tensor", "dp"),
            P(None, "tensor"),
            P(None, "tensor"),
            P(None, "tensor"),
            P(),
            P(),
            P(),
        ),
        check_vma=False,
    )
```

profile of v0, /device:TPU:0, one launch (start us, length us, event | category | flops | bytes accessed | tf_op | source)
XLA Modules:
  0.0 661.8 jit_solution(4477941152413452380)
XLA Ops:
  14.5 5.6 all-gather.1
  20.2 6.1 gather_fusion
  27.0 3.5 fusion.107
  33.8 40.4 %all-gather.5.cloned.1.call-done = bf16[1536,1152]{1,0:T(8,128)(2,1)} async-done(((bf16[48,1152]{1,0:T(8,128)(2,1)}), bf16[1536,1152]{1,0:T(8,128)(2,1)}) %all-gather.5.cloned.1.call-update) | async-done | bytes 3538960 | tf_op jit(solution)/shard_map/all_gather | solution.py:99
  74.2 4.8 fusion.68
  83.1 4.9 reshape.281
  88.0 5.7 fusion.72
  97.5 4.8 reshape.280
  102.3 3.2 reshape.275
  105.5 4.7 reshape.279
  110.2 3.7 reshape.273
  113.9 3.8 reshape.274
  117.7 4.7 fusion.53
  122.4 8.9 %fusion.109 = (f32[32,6,49]{2,1,0:T(8,128)S(1)}, f32[32,6,49,49]{2,3,1,0:T(8,128)S(1)}) fusion(f32[32,6,49,49]{2,3,1,0:T(8,128)S(1)} %fusion.53), kind=kOutput, calls=%fused_computation.231 | output fusion | flops 1844016 | bytes 3725568 | tf_op jit(solution)/shard_map/sub | solution.py:134
  137.8 5.2 convert_element_type.213
  143.0 3.5 fusion.45
  146.5 8.9 %fusion.110 = (f32[32,6,49]{2,1,0:T(8,128)S(1)}, f32[32,6,49,49]{2,3,1,0:T(8,128)S(1)}) fusion(f32[32,6,49,49]{2,3,1,0:T(8,128)S(1)} %fusion.45), kind=kOutput, calls=%fused_computation.232 | output fusion | flops 1844016 | bytes 3725568 | tf_op jit(solution)/shard_map/sub | solution.py:134
  160.2 4.6 convert_element_type.219
  167.6 3.2 fusion.111
  174.1 8.7 %multiply_convert_fusion = (bf16[1568,1536]{1,0:T(8,128)(2,1)}, f32[1568,1536]{1,0:T(8,128)}) fusion(f32[1536]{0:T(1024)S(1)} %add.329, bf16[1568,768]{1,0:T(8,128)(2,1)S(1)} %add_convert_fusion.1, bf16[2,768,3456]{2,1,0:T(8,128)(2,1)S(1)} %bitcast.204), kind=kOutput, calls=%fused_computation.21 | convolution fusion | flops 3713826816 | bytes 19226624 | tf_op jit(solution)/shard_map/dot_general | solution.py:151
  182.9 8.8 %multiply_convert_fusion.1 = (bf16[1568,1536]{1,0:T(8,128)(2,1)}, f32[1568,1536]{1,0:T(8,128)}) fusion(f32[1536]{0:T(1024)S(1)} %add.325, bf16[1568,768]{1,0:T(8,128)(2,1)S(1)} %add_convert_fusion.1, bf16[2,768,3456]{2,1,0:T(8,128)(2,1)S(1)} %bitcast.205), kind=kOutput, calls=%fused_computation.23 | convolution fusion | flops 3713826816 | bytes 19226624 | tf_op jit(solution)/shard_map/dot_general | solution.py:151
  191.7 11.1 %convert_reduce_fusion = (f32[1536]{0:T(1024)}, bf16[1568,1536]{1,0:T(8,128)(2,1)}) fusion(f32[1568,1536]{1,0:T(8,128)} %get-tuple-element.127, bf16[1568,768]{1,0:T(8,128)(2,1)S(1)} %copy-done.14, bf16[2,768,3456]{2,1,0:T(8,128)(2,1)S(1)} %bitcast.206), kind=kOutput, calls=%fused_computation.19 | convolution fusion | flops 3733092864 | bytes 19224576 | tf_op jit(solution)/shard_map/dot_general | solution.py:159
  202.8 9.4 %convert_reduce_fusion.1 = (f32[1536]{0:T(1024)}, bf16[1568,1536]{1,0:T(8,128)(2,1)S(1)}) fusion(f32[1568,1536]{1,0:T(8,128)} %get-tuple-element.125, bf16[1568,768]{1,0:T(8,128)(2,1)S(1)} %copy-done.14, bf16[2,768,3456]{2,1,0:T(8,128)(2,1)S(1)} %bitcast.207), kind=kOutput, calls=%fused_computation.20 | convolution fusion | flops 3733092864 | bytes 19224576 | tf_op jit(solution)/shard_map/dot_general | solution.py:159
  212.2 5.7 fusion.65
  218.0 9.9 %multiply_reduce_fusion.4 = (f32[768]{0:T(1024)S(1)}, f32[1568]{0:T(1024)S(1)}, f32[768]{0:T(1024)S(1)}, f32[1568,768]{1,0:T(8,128)S(1)}) fusion(f32[1568,768]{1,0:T(8,128)S(1)} %get-tuple-element.123, f32[1568]{0:T(1024)S(1)} %fusion.91, f32[1568]{0:T(1024)S(1)} %broadcast_multiply_fusion, f32[768]{0:T(1024)S(1)} %get-tuple-element.71, ...), kind=kOutput, calls=%fused_computation.50 | convolution fusion | flops 3710211072 | bytes 21654912 | tf_op jit(solution)/shard_map/dot_general | solution.py:43
  236.7 3.5 convolution_convert_fusion.6
  242.8 5.2 reshape.286
  248.0 6.5 multiply_reduce_fusion
  254.6 3.1 convert_reduce_fusion.3
  259.7 3.2 fusion.26
  262.9 3.3 convert_reduce_fusion.4
  266.1 3.3 reshape.282
  269.5 6.5 multiply_reduce_fusion.1
  284.2 3.2 convert_reduce_fusion.6
  314.7 7.0 %convolution_convert_fusion.1 = bf16[768,1152]{1,0:T(8,128)(2,1)} fusion(bf16[1568,768]{1,0:T(8,128)(2,1)S(1)} %copy-done.27, bf16[1568,1152]{1,0:T(8,128)(2,1)} %constant_dynamic-update-slice_fusion), kind=kOutput, calls=%fused_computation.69 | convolution fusion | flops 2775416832 | bytes 7790592 | tf_op jit(solution)/shard_map/dot_general | solution.py:37
  338.1 5.9 convolution_convert_fusion
  348.4 7.8 %convolution_convert_fusion.3 = bf16[768,1536]{1,0:T(8,128)(2,1)S(1)} fusion(bf16[1568,768]{1,0:T(8,128)(2,1)} %copy-done.29, bf16[1568,1536]{1,0:T(8,128)(2,1)} %get-tuple-element.135), kind=kOutput, calls=%fused_computation.71 | convolution fusion | flops 3700555776 | bytes 9584640 | tf_op jit(solution)/shard_map/dot_general | solution.py:37
  356.2 7.3 %fusion.22 = bf16[768,1536]{1,0:T(8,128)(2,1)S(1)} fusion(bf16[1568,1536]{1,0:T(8,128)(2,1)} %get-tuple-element.126, bf16[1568,768]{1,0:T(8,128)(2,1)S(1)} %copy-done.15), kind=kOutput, calls=%fused_computation.76 | convolution fusion | flops 3700555776 | bytes 9584640 | tf_op jit(solution)/shard_map/dot_general | solution.py:37
  366.5 4.8 convolution_convert_fusion.5
  371.4 5.0 fusion.21
  379.1 8.5 %pad_maximum_fusion = bf16[2,768,3072]{2,1,0:T(8,128)(2,1)} fusion(bf16[1,768,3072]{2,1,0:T(8,128)(2,1)} %maximum_bitcast_fusion.1, bf16[1,768,3072]{2,1,0:T(8,128)(2,1)} %maximum_bitcast_fusion), kind=kLoop, calls=%fused_computation.25 | loop fusion | flops 4718592 | bytes 18874368 | tf_op jit(solution)/shard_map/stack | solution.py:167
  388.8 8.3 %fusion.70 = f32[1568,768]{1,0:T(8,128)} fusion(bf16[1568,1152]{1,0:T(8,128)(2,1)} %constant_dynamic-update-slice_fusion, bf16[1536,1152]{1,0:T(8,128)(2,1)} %all-gather.5.cloned.1.call-done), kind=kOutput, calls=%fused_computation.136 | convolution fusion | flops 2774532096 | bytes 10199040 | tf_op jit(solution)/shard_map/dot_general | solution.py:43
  397.2 7.0 %multiply_reduce_fusion.5 = (f32[768]{0:T(1024)S(1)}, f32[1568]{0:T(1024)S(1)}, f32[768]{0:T(1024)S(1)}, f32[1568,768]{1,0:T(8,128)S(1)}) fusion(f32[1568,768]{1,0:T(8,128)S(1)} %bitcast.176, f32[1568]{0:T(1024)S(1)} %copy-done.50, f32[1568]{0:T(1024)S(1)} %copy-done.42, f32[768]{0:T(1024)S(1)} %copy-done.54, f32[1568,768]{1,0:T(8,128)} %fusion.70, ...), kind=kOutput, calls=%fused_computation.52 | convolution fusion | flops 2785367040 | bytes 19865728 | tf_op jit(solution)/shard_map/dot_general | solution.py:43
  409.1 7.0 %fusion.66 = f32[1568,768]{1,0:T(8,128)S(1)} fusion(bf16[1568,1536]{1,0:T(8,128)(2,1)} %get-tuple-element.124, bf16[2,768,3456]{2,1,0:T(8,128)(2,1)} %bitcast.200), kind=kOutput, calls=%fused_computation.132 | convolution fusion | flops 3699376128 | bytes 11993088 | tf_op jit(solution)/shard_map/dot_general | solution.py:43
  416.1 8.7 %add_convert_fusion = bf16[1568,768]{1,0:T(8,128)(2,1)} fusion(f32[1568,768]{1,0:T(8,128)S(1)} %bitcast.178, f32[1568,768]{1,0:T(8,128)S(1)} %fusion.66, bf16[1568,1536]{1,0:T(8,128)(2,1)} %get-tuple-element.126, f32[768]{0:T(1024)S(1)} %copy-done.57, bf16[2,768,3456]{2,1,0:T(8,128)(2,1)} %bitcast.201), kind=kOutput, calls=%fused_computation.56 | convolution fusion | flops 3704193024 | bytes 19221504 | tf_op jit(solution)/shard_map/dot_general | solution.py:43
  424.8 29.5 %reduce-scatter.3.cloned.1.call-done = bf16[48,1536]{1,0:T(8,128)(2,1)} async-done(((bf16[1536,1536]{1,0:T(8,128)(2,1)}), bf16[48,1536]{1,0:T(8,128)(2,1)}) %reduce-scatter.3.cloned.1.call-update) | async-done | bytes 147472 | tf_op jit(solution)/shard_map/reduce_scatter | solution.py:168
  455.9 139.4 %reduce-scatter.5.cloned.1.call-done = bf16[48,3072]{1,0:T(8,128)(2,1)} async-done(((bf16[1536,3072]{1,0:T(8,128)(2,1)}), bf16[48,3072]{1,0:T(8,128)(2,1)}) %reduce-scatter.5.cloned.1.call-update) | async-done | bytes 294928 | tf_op jit(solution)/shard_map/reduce_scatter | solution.py:168
  599.2 40.4 %all-reduce = (f32[]{:T(128)}, f32[6,768]{1,0:T(8,128)S(1)}, f32[2,6,384]{2,1,0:T(8,128)S(1)}) all-reduce(f32[]{:T(128)S(6)} %add.344, f32[6,768]{1,0:T(8,128)S(1)} %stack.60, f32[2,6,384]{2,1,0:T(8,128)S(1)} %pad_maximum_fusion.3), channel_id=1, replica_groups=mesh['dp'=16,'tensor'=2] {'dp','tensor'}, use_global_device_ids=true, to_apply=%region_18.19 | all-reduce | flops 9217 | bytes 73736 | tf_op jit(solution)/shard_map/psum | solution.py:248
  (284 shorter events, 133.2 us)
Async XLA Ops:
  7.2 13.0 %copy-start = (f32[196,768]{1,0:T(8,128)S(1)}, f32[196,768]{1,0:T(8,128)}, u32[]{:S(2)}) copy-start(f32[196,768]{1,0:T(8,128)} %param.25) | copy-start | bytes 1806340
  7.2 66.9 %all-gather.5.cloned.1.call-start = ((), (), s32[]{:S(2)}) async-start(), calls=%async_computation.2 | async-start | bytes 3649536 | tf_op jit(solution)/shard_map/all_gather | solution.py:99
  8.9 155.9 %all-gather.7.cloned.1.call-start = ((), (), s32[]{:S(2)}) async-start(), calls=%async_computation.3 | async-start | bytes 10948608 | tf_op jit(solution)/shard_map/all_gather | solution.py:99
  12.8 441.6 %reduce-scatter.3.cloned.1.call-start = ((), (), s32[]{:S(2)}) async-start(), calls=%async_computation.4 | async-start | bytes 4866048 | tf_op jit(solution)/shard_map/reduce_scatter | solution.py:168
  20.2 6.8 %copy-start.25 = (bf16[1568,768]{1,0:T(8,128)(2,1)S(1)}, bf16[1568,768]{1,0:T(8,128)(2,1)}, u32[]{:S(2)}) copy-start(bf16[1568,768]{1,0:T(8,128)(2,1)} %param.23) | copy-start | bytes 7225348
  33.8 45.2 %copy-start.26 = (bf16[1568,768]{1,0:T(8,128)(2,1)}, bf16[1568,768]{1,0:T(8,128)(2,1)S(1)}, u32[]{:S(2)}) copy-start(bf16[1568,768]{1,0:T(8,128)(2,1)S(1)} %add_convert_fusion.2) | copy-start | bytes 7225348
  83.1 11.8 %slice-start.12 = ((s8[7225344]{0:T(1024)(128)(4,1)}), s8[3031040]{0:T(1024)(128)(4,1)S(1)}, s32[]{:S(2)}) async-start(s8[7225344]{0:T(1024)(128)(4,1)} %bitcast.187), calls=%async_computation.18 | async-start | bytes 6062080
  88.0 6.9 %slice-start.13 = ((s8[7225344]{0:T(1024)(128)(4,1)}), s8[4194304]{0:T(1024)(128)(4,1)S(1)}, s32[]{:S(2)}) async-start(s8[7225344]{0:T(1024)(128)(4,1)} %bitcast.187), calls=%async_computation.19 | async-start | bytes 8388608
  102.3 7.9 %copy-start.19 = (bf16[1568,384]{1,0:T(8,128)(2,1)S(1)}, bf16[1568,384]{1,0:T(8,128)(2,1)}, u32[]{:S(2)}) copy-start(bf16[1568,384]{1,0:T(8,128)(2,1)} %get-tuple-element.146) | copy-start | bytes 3612676
  122.4 11.3 %copy-start.20 = (bf16[32,49,6,64]{3,2,1,0:T(8,128)(2,1)S(1)}, bf16[32,49,6,64]{3,2,1,0:T(8,128)(2,1)}, u32[]{:S(2)}) copy-start(bf16[32,49,6,64]{3,2,1,0:T(8,128)(2,1)} %reshape.273) | copy-start | bytes 3612676
  135.4 7.6 %copy-start.7 = (bf16[32,49,6,64]{3,2,1,0:T(8,128)(2,1)S(1)}, bf16[32,49,6,64]{3,2,1,0:T(8,128)(2,1)}, u32[]{:S(2)}) copy-start(bf16[32,49,6,64]{3,2,1,0:T(8,128)(2,1)} %reshape.280) | copy-start | bytes 3612676
  146.5 9.0 %copy-start.21 = (bf16[32,49,6,64]{3,2,1,0:T(8,128)(2,1)S(1)}, bf16[32,49,6,64]{3,2,1,0:T(8,128)(2,1)}, u32[]{:S(2)}) copy-start(bf16[32,49,6,64]{3,2,1,0:T(8,128)(2,1)} %reshape.279) | copy-start | bytes 3612676
  157.8 7.1 %copy-start.16 = (bf16[1568,384]{1,0:T(8,128)(2,1)S(1)}, bf16[1568,384]{1,0:T(8,128)(2,1)}, u32[]{:S(2)}) copy-start(bf16[1568,384]{1,0:T(8,128)(2,1)} %convert_element_type.213) | copy-start | bytes 3612676
  160.2 7.3 %slice-start = ((s8[4816896]{0:T(1024)(128)(4,1)}), s8[622592]{0:T(1024)(128)(4,1)S(1)}, s32[]{:S(2)}) async-start(s8[4816896]{0:T(1024)(128)(4,1)} %bitcast.173), calls=%async_computation.6 | async-start | bytes 1245184
  170.8 57.1 %copy-start.3 = (f32[1568,768]{1,0:T(8,128)}, f32[1568,768]{1,0:T(8,128)S(1)}, u32[]{:S(2)}) copy-start(f32[1568,768]{1,0:T(8,128)S(1)} %get-tuple-element.123) | copy-start | bytes 14450692
  174.1 8.7 %copy-start.29 = (bf16[1568,768]{1,0:T(8,128)(2,1)}, bf16[1568,768]{1,0:T(8,128)(2,1)S(1)}, u32[]{:S(2)}) copy-start(bf16[1568,768]{1,0:T(8,128)(2,1)S(1)} %add_convert_fusion.1) | copy-start | bytes 7225348
  182.9 8.8 %copy-start.14 = (bf16[1568,768]{1,0:T(8,128)(2,1)S(1)}, bf16[1568,768]{1,0:T(8,128)(2,1)}, u32[]{:S(2)}) copy-start(bf16[1568,768]{1,0:T(8,128)(2,1)} %param.26) | copy-start | bytes 7225348
  242.8 11.7 %slice-start.10 = ((s8[5505024]{0:T(1024)(128)(4,1)}), s8[1310720]{0:T(1024)(128)(4,1)S(1)}, s32[]{:S(2)}) async-start(s8[5505024]{0:T(1024)(128)(4,1)} %bitcast.184), calls=%async_computation.16 | async-start | bytes 2621440
  262.9 13.1 %slice-start.8 = ((s8[5505024]{0:T(1024)(128)(4,1)}), s8[1310720]{0:T(1024)(128)(4,1)S(1)}, s32[]{:S(2)}) async-start(s8[5505024]{0:T(1024)(128)(4,1)} %bitcast.182), calls=%async_computation.14 | async-start | bytes 2621440
  269.4 6.6 %copy-start.23 = (bf16[32,49,6,64]{3,2,1,0:T(8,128)(2,1)S(1)}, bf16[32,49,6,64]{3,2,1,0:T(8,128)(2,1)}, u32[]{:S(2)}) copy-start(bf16[32,49,6,64]{3,2,1,0:T(8,128)(2,1)} %reshape.282) | copy-start | bytes 3612676
  314.7 7.0 %copy-start.24 = (bf16[32,49,6,64]{3,1,2,0:T(8,128)(2,1)S(1)}, bf16[32,49,6,64]{3,1,2,0:T(8,128)(2,1)}, u32[]{:S(2)}) copy-start(bf16[32,49,6,64]{3,1,2,0:T(8,128)(2,1)} %get-tuple-element.139) | copy-start | bytes 3612676
  347.9 8.3 %copy-start.15 = (bf16[1568,768]{1,0:T(8,128)(2,1)S(1)}, bf16[1568,768]{1,0:T(8,128)(2,1)}, u32[]{:S(2)}) copy-start(bf16[1568,768]{1,0:T(8,128)(2,1)} %param.26) | copy-start | bytes 7225348
  347.9 247.4 %reduce-scatter.5.cloned.1.call-start = ((), (), s32[]{:S(2)}) async-start(), calls=%async_computation.5 | async-start | bytes 9732096 | tf_op jit(solution)/shard_map/reduce_scatter | solution.py:168
  348.3 18.2 %slice-start.17 = ((s8[4816896]{0:T(1024)(128)(4,1)}), s8[4194304]{0:T(1024)(128)(4,1)S(1)}, s32[]{:S(2)}) async-start(s8[4816896]{0:T(1024)(128)(4,1)} %bitcast.210), calls=%async_computation.23 | async-start | bytes 8388608
  356.2 10.3 %slice-start.18 = ((s8[4816896]{0:T(1024)(128)(4,1)}), s8[622592]{0:T(1024)(128)(4,1)S(1)}, s32[]{:S(2)}) async-start(s8[4816896]{0:T(1024)(128)(4,1)} %bitcast.210), calls=%async_computation.24 | async-start | bytes 1245184
  363.5 7.9 %slice-start.19 = ((s8[4816896]{0:T(1024)(128)(4,1)}), s8[4194304]{0:T(1024)(128)(4,1)S(1)}, s32[]{:S(2)}) async-start(s8[4816896]{0:T(1024)(128)(4,1)} %bitcast.212), calls=%async_computation.25 | async-start | bytes 8388608
  387.5 9.6 %slice-start.2 = ((s8[4816896]{0:T(1024)(128)(4,1)}), s8[622592]{0:T(1024)(128)(4,1)S(1)}, s32[]{:S(2)}) async-start(s8[4816896]{0:T(1024)(128)(4,1)} %bitcast.175), calls=%async_computation.8 | async-start | bytes 1245184
  388.8 8.3 %slice-start.3 = ((s8[4816896]{0:T(1024)(128)(4,1)}), s8[4194304]{0:T(1024)(128)(4,1)S(1)}, s32[]{:S(2)}) async-start(s8[4816896]{0:T(1024)(128)(4,1)} %bitcast.175), calls=%async_computation.9 | async-start | bytes 8388608
  388.8 8.3 %copy-start.37 = (bf16[1568,1152]{1,0:T(8,128)(2,1)S(1)}, bf16[1568,1152]{1,0:T(8,128)(2,1)}, u32[]{:S(2)}) copy-start(bf16[1568,1152]{1,0:T(8,128)(2,1)} %constant_dynamic-update-slice_fusion.3) | copy-start | bytes 10838020
  388.8 8.3 %copy-start.42 = (f32[1568]{0:T(1024)S(1)}, f32[1568]{0:T(1024)}, u32[]{:S(2)}) copy-start(f32[1568]{0:T(1024)} %copy-done.41) | copy-start | bytes 18820
  388.8 8.4 %copy-start.50 = (f32[1568]{0:T(1024)S(1)}, f32[1568]{0:T(1024)}, u32[]{:S(2)}) copy-start(f32[1568]{0:T(1024)} %copy-done.49) | copy-start | bytes 18820
  388.8 8.4 %copy-start.54 = (f32[768]{0:T(1024)S(1)}, f32[768]{0:T(1024)}, u32[]{:S(2)}) copy-start(f32[768]{0:T(1024)} %copy-done.53) | copy-start | bytes 9220
  388.8 8.4 %copy-start.58 = (bf16[1536,1152]{1,0:T(8,128)(2,1)S(1)}, bf16[1536,1152]{1,0:T(8,128)(2,1)}, u32[]{:S(2)}) copy-start(bf16[1536,1152]{1,0:T(8,128)(2,1)} %all-gather.5.cloned.1.call-done) | copy-start | bytes 10616836
  388.8 17.2 %slice-start.6 = ((s8[4816896]{0:T(1024)(128)(4,1)}), s8[4194304]{0:T(1024)(128)(4,1)S(1)}, s32[]{:S(2)}) async-start(s8[4816896]{0:T(1024)(128)(4,1)} %bitcast.179), calls=%async_computation.12 | async-start | bytes 8388608
  397.2 7.0 %copy-start.48 = (f32[1568]{0:T(1024)S(1)}, f32[1568]{0:T(1024)}, u32[]{:S(2)}) copy-start(f32[1568]{0:T(1024)} %copy-done.47) | copy-start | bytes 18820
  397.2 8.8 %slice-start.7 = ((s8[4816896]{0:T(1024)(128)(4,1)}), s8[622592]{0:T(1024)(128)(4,1)S(1)}, s32[]{:S(2)}) async-start(s8[4816896]{0:T(1024)(128)(4,1)} %bitcast.179), calls=%async_computation.13 | async-start | bytes 1245184
  406.0 10.0 %slice-start.4 = ((s8[4816896]{0:T(1024)(128)(4,1)}), s8[622592]{0:T(1024)(128)(4,1)S(1)}, s32[]{:S(2)}) async-start(s8[4816896]{0:T(1024)(128)(4,1)} %bitcast.177), calls=%async_computation.10 | async-start | bytes 1245184
  409.1 7.0 %slice-start.5 = ((s8[4816896]{0:T(1024)(128)(4,1)}), s8[4194304]{0:T(1024)(128)(4,1)S(1)}, s32[]{:S(2)}) async-start(s8[4816896]{0:T(1024)(128)(4,1)} %bitcast.177), calls=%async_computation.11 | async-start | bytes 8388608
  409.1 7.0 %copy-start.57 = (f32[768]{0:T(1024)S(1)}, f32[768]{0:T(1024)}, u32[]{:S(2)}) copy-start(f32[768]{0:T(1024)} %get-tuple-element.69) | copy-start | bytes 9220
  416.1 228.1 %copy-start.44 = (f32[6,768]{1,0:T(8,128)S(1)}, f32[6,768]{1,0:T(8,128)}, u32[]{:S(2)}) copy-start(f32[6,768]{1,0:T(8,128)} %param.43) | copy-start | bytes 55300
  416.1 229.5 %copy-start.40 = (f32[384,48]{0,1:T(8,128)S(1)}, f32[384,48]{0,1:T(8,128)}, u32[]{:S(2)}) copy-start(f32[384,48]{0,1:T(8,128)} %param.31) | copy-start | bytes 221188
  424.8 222.4 %copy-start.52 = (f32[6,384]{1,0:T(8,128)S(1)}, f32[6,384]{1,0:T(8,128)}, u32[]{:S(2)}) copy-start(f32[6,384]{1,0:T(8,128)} %param.40) | copy-start | bytes 27652
  424.8 223.8 %copy-start.34 = (f32[48,3,384]{2,0,1:T(8,128)S(1)}, f32[48,3,384]{2,0,1:T(8,128)}, u32[]{:S(2)}) copy-start(f32[48,3,384]{2,0,1:T(8,128)} %param.28) | copy-start | bytes 663556
  424.8 225.7 %copy-start.32 = (f32[48,4,384]{2,1,0:T(4,128)S(1)}, f32[48,4,384]{2,1,0:T(4,128)}, u32[]{:S(2)}) copy-start(f32[48,4,384]{2,1,0:T(4,128)} %param.34) | copy-start | bytes 884740
  424.8 225.7 %copy-start.38 = (f32[48,4,384]{2,1,0:T(4,128)S(1)}, f32[48,4,384]{2,1,0:T(4,128)}, u32[]{:S(2)}) copy-start(f32[48,4,384]{2,1,0:T(4,128)} %param.36) | copy-start | bytes 884740
  424.8 225.7 %copy-start.39 = (f32[48,4,384]{2,1,0:T(4,128)S(1)}, f32[48,4,384]{2,1,0:T(4,128)}, u32[]{:S(2)}) copy-start(f32[48,4,384]{2,1,0:T(4,128)} %param.35) | copy-start | bytes 884740
  424.8 227.0 %copy-start.33 = (f32[4,384,48]{1,2,0:T(8,128)S(1)}, f32[4,384,48]{1,2,0:T(8,128)}, u32[]{:S(2)}) copy-start(f32[4,384,48]{1,2,0:T(8,128)} %param.37) | copy-start | bytes 884740
  642.9 11.1 %copy-start.1 = (f32[196,768]{1,0:T(8,128)S(1)}, f32[196,768]{1,0:T(8,128)}, u32[]{:S(2)}) copy-start(f32[196,768]{1,0:T(8,128)} %param.25) | copy-start | bytes 1806340
  (37 other events, 134.0 us)
Sparse Core Ops, SparseCore 0:
  11.5 62.6 all-gather.4
  77.1 85.3 all-gather.6
  348.0 106.2 reduce-scatter.2
  460.1 135.1 reduce-scatter.4
where the time goes:
time: 673 us; the launch traced here: 662 us
  waiting for transfers between devices  209 us (31%)
  matrix products  193 us (29%)
  local copies, waits for them, and re-layouts  116 us (17%)
  other arithmetic  76.6 us (11%)
  blocking collectives  46 us (7%)
  between operations  20.5 us (3%)
    reduce_scatter x2, waiting for transfers between devices, scatter(): lax.psum_scatter(stacked, every, scatter_dimension=0, tiled=True)  169 us
    dot_general x8, matrix products, dot_back(): lax.dot_general(left_side, right_side, (((1,), (1,)), ((), ())), preferre...  52.4 us
    dot_general x8, matrix products, transpose_dot(): lax.dot_general(left_side, right_side, (((0,), (0,)), ((), ())), preferre...  42.7 us
    psum x1, blocking collectives, body(): lax.psum((grad_norm_rows, grad_split, local_square), ('dp', 'tensor'))  40.4 us
    all_gather x2, waiting for transfers between devices, gather(): whole = lax.all_gather(block.astype(low_type), every, axis=0, tiled=True)  40.4 us
    unnamed x167, local copies, waits for them, and re-layouts  22.2 us
    dot_general x2, matrix products, body(): jnp.dot(cotangent, fc2_low[t], preferred_element_type=jnp.float32)  20.5 us
    sub x2, other arithmetic, body(): attention = jax.nn.softmax(scores, axis=-1)  17.9 us
  transfers between devices with their start and end apart: 4, of which 3 were waited for; matrix products, arithmetic and copies ran while one was open for 27% of the time, Pallas kernels for 0%

commit v1 on v0

--- a/solution.py
+++ b/solution.py
@@ -96,7 +96,10 @@
         return jnp.swapaxes(proj_like, -1, -2)
 
     def gather(block):
-        whole = lax.all_gather(block.astype(low_type), every, axis=0, tiled=True)
+        whole = jnp.concatenate(
+            lax.all_to_all(jnp.stack([block.astype(low_type)] * lax.axis_size(every)), every, 0, 0),
+            axis=0,
+        )
         return whole.reshape(halves, model_width, block.shape[1])
 
     fc2_rows = jnp.transpose(w_fc2, (2, 0, 1)).reshape(shard_rows, 4 * shard_width)

time: 673 us -> 857 us (1.27)
  waiting for transfers between devices: 209 us -> 312 us
  blocking collectives: 46 us -> 109 us
  starting transfers between devices: 0.57 us -> 11.6 us
  local copies, waits for them, and re-layouts: 116 us -> 125 us
    all_to_all x0 -> x2, waiting for transfers between devices: none -> 144 us  [gather(): lax.all_to_all(jnp.stack([block.astype(low_type)] * lax.axis_size(every))...]
    all_gather x1, blocking collectives: 5.6 us -> 68.9 us  [body(): split_whole_bias = lax.all_gather(split_bias, 'tensor', axis=0, tiled=False)]
    all_gather x2 -> x0, waiting for transfers between devices: 40.4 us -> none  [gather(): whole = lax.all_gather(block.astype(low_type), every, axis=0, tiled=True)]
    all_to_all x0 -> x2, starting transfers between devices: none -> 11.3 us  [gather(): lax.all_to_all(jnp.stack([block.astype(low_type)] * lax.axis_size(every))...]
    unnamed x167 -> x169, local copies, waits for them, and re-layouts: 22.2 us -> 12.5 us
  transfers between devices with their start and end apart: 4 -> 4, of which waited for: 3 -> 4; matrix products, arithmetic and copies ran while one was open for 27% -> 20% of each run, Pallas kernels for 0% -> 0%
where the time goes in v1:
time: 857 us; the launch traced here: 845 us
  waiting for transfers between devices  312 us (36%)
  matrix products  191 us (22%)
  local copies, waits for them, and re-layouts  125 us (15%)
  blocking collectives  109 us (13%)
  other arithmetic  75.2 us (9%)
  between operations  21.2 us (2%)
  starting transfers between devices  11.6 us (1%)
    reduce_scatter x2, waiting for transfers between devices, scatter(): lax.psum_scatter(stacked, every, scatter_dimension=0, tiled=True)  168 us
    all_to_all x2, waiting for transfers between devices, gather(): lax.all_to_all(jnp.stack([block.astype(low_type)] * lax.axis_size(every))...  144 us
    all_gather x1, blocking collectives, body(): split_whole_bias = lax.all_gather(split_bias, 'tensor', axis=0, tiled=False)  68.9 us
    dot_general x8, matrix products, dot_back(): lax.dot_general(left_side, right_side, (((1,), (1,)), ((), ())), preferre...  52.9 us
    dot_general x8, matrix products, transpose_dot(): lax.dot_general(left_side, right_side, (((0,), (0,)), ((), ())), preferre...  41.9 us
    psum x1, blocking collectives, body(): lax.psum((grad_norm_rows, grad_split, local_square), ('dp', 'tensor'))  40.4 us
    dot_general x2, matrix products, body(): jnp.dot(cotangent, fc2_low[t], preferred_element_type=jnp.float32)  20.5 us
    dot_general x2, matrix products, body(): jnp.dot(normed_two_low, fc1_low[t], preferred_element_type=jnp.float32)  18 us
  transfers between devices with their start and end apart: 4, of which 4 were waited for; matrix products, arithmetic and copies ran while one was open for 20% of the time, Pallas kernels for 0%

profile of v1, /device:TPU:0, one launch (start us, length us, event | category | flops | bytes accessed | tf_op | source)
XLA Modules:
  0.0 845.4 jit_solution(16880304775108819399)
XLA Ops:
  10.3 7.4 all-to-all-start
  18.0 80.6 %all-to-all-done = bf16[32,48,1152]{2,1,0:T(8,128)(2,1)} async-done(((bf16[32,48,1152]{2,1,0:T(8,128)(2,1)}), bf16[32,48,1152]{2,1,0:T(8,128)(2,1)}, u32[]{:S(2)}, u32[]{:S(2)}) %all-to-all-start) | async-done | bytes 3538976 | tf_op jit(solution)/shard_map/all_to_all | solution.py:100
  98.5 4.6 stack.37
  107.3 68.9 %all-gather.1 = f32[2,6,384]{2,1,0:T(8,128)S(1)} all-gather(f32[1,6,384]{2,1,0:T(8,128)S(1)} %bitcast.203), channel_id=2, replica_groups=mesh['dp'=16,'tensor'=2] {'tensor'}, dimensions={0}, use_global_device_ids=true | all-gather | bytes 27648 | tf_op jit(solution)/shard_map/all_gather | solution.py:115
  176.3 6.1 gather_fusion
  188.9 4.4 fusion.101
  202.9 5.7 fusion.106
  211.1 4.7 reshape.284
  219.0 4.8 reshape.283
  230.3 4.5 fusion.53
  234.8 8.9 %fusion.103 = (f32[32,6,49]{2,1,0:T(8,128)S(1)}, f32[32,6,49,49]{2,3,1,0:T(8,128)S(1)}) fusion(f32[32,6,49,49]{2,3,1,0:T(8,128)S(1)} %fusion.53), kind=kOutput, calls=%fused_computation.225 | output fusion | flops 1844016 | bytes 3725568 | tf_op jit(solution)/shard_map/sub | solution.py:137
  248.5 4.3 convert_element_type.217
  252.8 4.5 fusion.45
  257.3 8.9 %fusion.104 = (f32[32,6,49]{2,1,0:T(8,128)S(1)}, f32[32,6,49,49]{2,3,1,0:T(8,128)S(1)}) fusion(f32[32,6,49,49]{2,3,1,0:T(8,128)S(1)} %fusion.45), kind=kOutput, calls=%fused_computation.226 | output fusion | flops 1844016 | bytes 3725568 | tf_op jit(solution)/shard_map/sub | solution.py:137
  271.0 5.4 convert_element_type.223
  276.4 63.4 %all-to-all-done.1 = bf16[32,48,3456]{2,1,0:T(8,128)(2,1)} async-done(((bf16[32,48,3456]{2,1,0:T(8,128)(2,1)}), bf16[32,48,3456]{2,1,0:T(8,128)(2,1)}, u32[]{:S(2)}, u32[]{:S(2)}) %all-to-all-start.1) | async-done | bytes 10616864 | tf_op jit(solution)/shard_map/all_to_all | solution.py:100
  347.5 8.5 %multiply_convert_fusion = (bf16[1568,1536]{1,0:T(8,128)(2,1)}, f32[1568,1536]{1,0:T(8,128)S(1)}) fusion(f32[1536]{0:T(1024)S(1)} %add.329, bf16[1568,768]{1,0:T(8,128)(2,1)S(1)} %add_convert_fusion.1, bf16[2,768,3456]{2,1,0:T(8,128)(2,1)} %bitcast.5), kind=kOutput, calls=%fused_computation.21 | convolution fusion | flops 3713826816 | bytes 19224576 | tf_op jit(solution)/shard_map/dot_general | solution.py:154
  356.0 9.5 %multiply_convert_fusion.1 = (bf16[1568,1536]{1,0:T(8,128)(2,1)}, f32[1568,1536]{1,0:T(8,128)}) fusion(f32[1536]{0:T(1024)S(1)} %add.325, bf16[1568,768]{1,0:T(8,128)(2,1)S(1)} %add_convert_fusion.1, bf16[2,768,3456]{2,1,0:T(8,128)(2,1)} %bitcast.5), kind=kOutput, calls=%fused_computation.23 | convolution fusion | flops 3713826816 | bytes 19224576 | tf_op jit(solution)/shard_map/dot_general | solution.py:154
  365.5 10.3 %convert_reduce_fusion = (f32[1536]{0:T(1024)}, bf16[1568,1536]{1,0:T(8,128)(2,1)}) fusion(f32[1568,1536]{1,0:T(8,128)S(1)} %get-tuple-element.129, bf16[1568,768]{1,0:T(8,128)(2,1)S(1)} %copy-done.12, bf16[2,768,3456]{2,1,0:T(8,128)(2,1)} %bitcast.5), kind=kOutput, calls=%fused_computation.19 | convolution fusion | flops 3733092864 | bytes 19224576 | tf_op jit(solution)/shard_map/dot_general | solution.py:162
  375.9 10.1 %convert_reduce_fusion.1 = (f32[1536]{0:T(1024)}, bf16[1568,1536]{1,0:T(8,128)(2,1)S(1)}) fusion(f32[1568,1536]{1,0:T(8,128)} %get-tuple-element.127, bf16[1568,768]{1,0:T(8,128)(2,1)S(1)} %copy-done.12, bf16[2,768,3456]{2,1,0:T(8,128)(2,1)} %bitcast.5), kind=kOutput, calls=%fused_computation.20 | convolution fusion | flops 3733092864 | bytes 19224576 | tf_op jit(solution)/shard_map/dot_general | solution.py:162
  386.0 8.9 %fusion.65 = f32[1568,768]{1,0:T(8,128)} fusion(bf16[1568,1536]{1,0:T(8,128)(2,1)S(1)} %get-tuple-element.143, bf16[2,768,3456]{2,1,0:T(8,128)(2,1)} %bitcast.5), kind=kOutput, calls=%fused_computation.131 | convolution fusion | flops 3699376128 | bytes 11993088 | tf_op jit(solution)/shard_map/dot_general | solution.py:43
  394.9 9.9 %multiply_reduce_fusion.4 = (f32[768]{0:T(1024)S(1)}, f32[1568]{0:T(1024)S(1)}, f32[768]{0:T(1024)S(1)}, f32[1568,768]{1,0:T(8,128)S(1)}) fusion(f32[1568,768]{1,0:T(8,128)S(1)} %get-tuple-element.125, f32[1568]{0:T(1024)S(1)} %fusion.84, f32[1568]{0:T(1024)S(1)} %broadcast_multiply_fusion, f32[768]{0:T(1024)S(1)} %get-tuple-element.71, ...), kind=kOutput, calls=%fused_computation.50 | convolution fusion | flops 3710211072 | bytes 21654912 | tf_op jit(solution)/shard_map/dot_general | solution.py:43
  419.0 5.0 reshape.290
  424.0 6.5 multiply_reduce_fusion
  445.4 6.5 multiply_reduce_fusion.1
  464.5 5.2 reshape.292
  472.0 4.3 reshape.288
  480.4 4.7 reshape.287
  486.3 4.1 copy.187
  490.4 4.3 reshape.289
  497.2 7.0 convolution_convert_fusion.1
  506.5 4.3 reshape.291
  512.1 4.2 copy.196
  516.2 4.3 reshape.293
  523.0 5.9 convolution_convert_fusion
  532.1 7.8 convolution_convert_fusion.3
  539.9 7.3 fusion.22
  550.2 4.8 convolution_convert_fusion.5
  555.1 5.0 fusion.21
  562.8 8.4 pad_maximum_fusion
  572.8 5.6 fusion.108
  578.5 6.8 multiply_reduce_fusion.5
  585.3 4.3 fusion.98
  592.7 7.0 fusion.66
  599.8 9.0 %add_convert_fusion = bf16[1568,768]{1,0:T(8,128)(2,1)} fusion(f32[1568,768]{1,0:T(8,128)S(1)} %bitcast.184, f32[1568,768]{1,0:T(8,128)S(1)} %fusion.66, bf16[1568,1536]{1,0:T(8,128)(2,1)} %get-tuple-element.128, f32[768]{0:T(1024)S(1)} %copy-done.64, bf16[2,768,3456]{2,1,0:T(8,128)(2,1)} %bitcast.5), kind=kOutput, calls=%fused_computation.56 | convolution fusion | flops 3704193024 | bytes 19221504 | tf_op jit(solution)/shard_map/dot_general | solution.py:43
  608.8 28.4 %reduce-scatter.3.cloned.1.call-done = bf16[48,1536]{1,0:T(8,128)(2,1)} async-done(((bf16[1536,1536]{1,0:T(8,128)(2,1)}), bf16[48,1536]{1,0:T(8,128)(2,1)}) %reduce-scatter.3.cloned.1.call-update) | async-done | bytes 147472 | tf_op jit(solution)/shard_map/reduce_scatter | solution.py:171
  638.8 139.5 %reduce-scatter.5.cloned.1.call-done = bf16[48,3072]{1,0:T(8,128)(2,1)} async-done(((bf16[1536,3072]{1,0:T(8,128)(2,1)}), bf16[48,3072]{1,0:T(8,128)(2,1)}) %reduce-scatter.5.cloned.1.call-update) | async-done | bytes 294928 | tf_op jit(solution)/shard_map/reduce_scatter | solution.py:171
  782.3 40.4 %all-reduce = (f32[]{:T(128)}, f32[6,768]{1,0:T(8,128)S(1)}, f32[2,6,384]{2,1,0:T(8,128)S(1)}) all-reduce(f32[]{:T(128)S(6)} %add.344, f32[6,768]{1,0:T(8,128)S(1)} %stack.46, f32[2,6,384]{2,1,0:T(8,128)S(1)} %pad_maximum_fusion.3), channel_id=1, replica_groups=mesh['dp'=16,'tensor'=2] {'dp','tensor'}, use_global_device_ids=true, to_apply=%region_18.19 | all-reduce | flops 9217 | bytes 73736 | tf_op jit(solution)/shard_map/psum | solution.py:251
  (285 shorter events, 138.9 us)
Async XLA Ops:
  7.2 169.1 %copy-start = (f32[196,768]{1,0:T(8,128)S(1)}, f32[196,768]{1,0:T(8,128)}, u32[]{:S(2)}) copy-start(f32[196,768]{1,0:T(8,128)} %param.25) | copy-start | bytes 1806340
  8.2 9.5 %copy-start.35 = (f32[48,4,384]{2,1,0:T(4,128)S(1)}, f32[48,4,384]{2,1,0:T(4,128)}, u32[]{:S(2)}) copy-start(f32[48,4,384]{2,1,0:T(4,128)} %param.34) | copy-start | bytes 884740
  10.3 7.6 copy-start.37
  10.3 7.6 copy-start.44
  10.3 88.2 %all-to-all-start = ((bf16[32,48,1152]{2,1,0:T(8,128)(2,1)}), bf16[32,48,1152]{2,1,0:T(8,128)(2,1)}, u32[]{:S(2)}, u32[]{:S(2)}) async-start(bf16[32,48,1152]{2,1,0:T(8,128)(2,1)} %stack.36), calls=%async_computation | async-start | bytes 7077888 | tf_op jit(solution)/shard_map/all_to_all | solution.py:100
  103.2 236.7 %all-to-all-start.1 = ((bf16[32,48,3456]{2,1,0:T(8,128)(2,1)}), bf16[32,48,3456]{2,1,0:T(8,128)(2,1)}, u32[]{:S(2)}, u32[]{:S(2)}) async-start(bf16[32,48,3456]{2,1,0:T(8,128)(2,1)} %stack.37), calls=%async_computation.1 | async-start | bytes 21233664 | tf_op jit(solution)/shard_map/all_to_all | solution.py:100
  107.0 530.2 %reduce-scatter.3.cloned.1.call-start = ((), (), s32[]{:S(2)}) async-start(), calls=%async_computation.4 | async-start | bytes 4866048 | tf_op jit(solution)/shard_map/reduce_scatter | solution.py:171
  176.3 6.2 copy-start.48
  176.3 6.8 copy-start.25
  188.9 7.7 copy-start.26
  234.8 9.0 %copy-start.20 = (bf16[32,49,6,64]{3,2,1,0:T(8,128)(2,1)S(1)}, bf16[32,49,6,64]{3,2,1,0:T(8,128)(2,1)}, u32[]{:S(2)}) copy-start(bf16[32,49,6,64]{3,2,1,0:T(8,128)(2,1)} %reshape.280) | copy-start | bytes 3612676
  257.3 9.0 %copy-start.21 = (bf16[32,49,6,64]{3,2,1,0:T(8,128)(2,1)S(1)}, bf16[32,49,6,64]{3,2,1,0:T(8,128)(2,1)}, u32[]{:S(2)}) copy-start(bf16[32,49,6,64]{3,2,1,0:T(8,128)(2,1)} %reshape.283) | copy-start | bytes 3612676
  271.0 71.5 %slice-start = ((s8[4816896]{0:T(1024)(128)(4,1)}), s8[622592]{0:T(1024)(128)(4,1)S(1)}, s32[]{:S(2)}) async-start(s8[4816896]{0:T(1024)(128)(4,1)} %bitcast.179), calls=%async_computation.6 | async-start | bytes 1245184
  345.6 59.3 %copy-start.3 = (f32[1568,768]{1,0:T(8,128)}, f32[1568,768]{1,0:T(8,128)S(1)}, u32[]{:S(2)}) copy-start(f32[1568,768]{1,0:T(8,128)S(1)} %get-tuple-element.125) | copy-start | bytes 14450692
  347.5 8.5 %copy-start.29 = (bf16[1568,768]{1,0:T(8,128)(2,1)}, bf16[1568,768]{1,0:T(8,128)(2,1)S(1)}, u32[]{:S(2)}) copy-start(bf16[1568,768]{1,0:T(8,128)(2,1)S(1)} %add_convert_fusion.1) | copy-start | bytes 7225348
  356.0 9.5 %copy-start.12 = (bf16[1568,768]{1,0:T(8,128)(2,1)S(1)}, bf16[1568,768]{1,0:T(8,128)(2,1)}, u32[]{:S(2)}) copy-start(bf16[1568,768]{1,0:T(8,128)(2,1)} %param.26) | copy-start | bytes 7225348
  386.0 8.9 %copy-start.65 = (bf16[1568,1536]{1,0:T(8,128)(2,1)}, bf16[1568,1536]{1,0:T(8,128)(2,1)S(1)}, u32[]{:S(2)}) copy-start(bf16[1568,1536]{1,0:T(8,128)(2,1)S(1)} %get-tuple-element.143) | copy-start | bytes 14450692
  419.0 11.5 %slice-start.10 = ((s8[5505024]{0:T(1024)(128)(4,1)}), s8[1310720]{0:T(1024)(128)(4,1)S(1)}, s32[]{:S(2)}) async-start(s8[5505024]{0:T(1024)(128)(4,1)} %bitcast.190), calls=%async_computation.16 | async-start | bytes 2621440
  424.0 6.5 slice-start.11
  424.0 6.6 copy-start.22
  438.7 13.1 %slice-start.8 = ((s8[5505024]{0:T(1024)(128)(4,1)}), s8[1310720]{0:T(1024)(128)(4,1)S(1)}, s32[]{:S(2)}) async-start(s8[5505024]{0:T(1024)(128)(4,1)} %bitcast.188), calls=%async_computation.14 | async-start | bytes 2621440
  445.4 6.5 slice-start.9
  445.4 6.6 copy-start.23
  497.2 7.0 copy-start.24
  512.1 8.5 %copy-start.18 = (bf16[1568,384]{1,0:T(8,128)(2,1)S(1)}, bf16[1568,384]{1,0:T(8,128)(2,1)}, u32[]{:S(2)}) copy-start(bf16[1568,384]{1,0:T(8,128)(2,1)} %reshape.292) | copy-start | bytes 3612676
  523.0 6.0 copy-start.34
  523.0 6.0 copy-start.40
  531.8 8.0 copy-start.13
  531.9 246.5 %reduce-scatter.5.cloned.1.call-start = ((), (), s32[]{:S(2)}) async-start(), calls=%async_computation.5 | async-start | bytes 9732096 | tf_op jit(solution)/shard_map/reduce_scatter | solution.py:171
  532.1 18.1 %slice-start.12 = ((s8[4816896]{0:T(1024)(128)(4,1)}), s8[4194304]{0:T(1024)(128)(4,1)S(1)}, s32[]{:S(2)}) async-start(s8[4816896]{0:T(1024)(128)(4,1)} %bitcast.204), calls=%async_computation.18 | async-start | bytes 8388608
  539.9 10.3 %slice-start.13 = ((s8[4816896]{0:T(1024)(128)(4,1)}), s8[622592]{0:T(1024)(128)(4,1)S(1)}, s32[]{:S(2)}) async-start(s8[4816896]{0:T(1024)(128)(4,1)} %bitcast.204), calls=%async_computation.19 | async-start | bytes 1245184
  547.2 7.9 slice-start.14
  571.3 7.1 slice-start.2
  572.8 16.8 %slice-start.6 = ((s8[4816896]{0:T(1024)(128)(4,1)}), s8[4194304]{0:T(1024)(128)(4,1)S(1)}, s32[]{:S(2)}) async-start(s8[4816896]{0:T(1024)(128)(4,1)} %bitcast.185), calls=%async_computation.12 | async-start | bytes 8388608
  578.5 6.8 copy-start.53
  578.5 11.2 %slice-start.7 = ((s8[4816896]{0:T(1024)(128)(4,1)}), s8[622592]{0:T(1024)(128)(4,1)S(1)}, s32[]{:S(2)}) async-start(s8[4816896]{0:T(1024)(128)(4,1)} %bitcast.185), calls=%async_computation.13 | async-start | bytes 1245184
  589.7 10.0 %slice-start.4 = ((s8[4816896]{0:T(1024)(128)(4,1)}), s8[622592]{0:T(1024)(128)(4,1)S(1)}, s32[]{:S(2)}) async-start(s8[4816896]{0:T(1024)(128)(4,1)} %bitcast.183), calls=%async_computation.10 | async-start | bytes 1245184
  592.7 7.1 slice-start.5
  592.7 7.1 copy-start.64
  599.8 227.5 %copy-start.49 = (f32[6,768]{1,0:T(8,128)S(1)}, f32[6,768]{1,0:T(8,128)}, u32[]{:S(2)}) copy-start(f32[6,768]{1,0:T(8,128)} %param.43) | copy-start | bytes 55300
  599.8 228.9 %copy-start.45 = (f32[384,48]{0,1:T(8,128)S(1)}, f32[384,48]{0,1:T(8,128)}, u32[]{:S(2)}) copy-start(f32[384,48]{0,1:T(8,128)} %param.31) | copy-start | bytes 221188
  608.8 221.5 %copy-start.59 = (f32[6,384]{1,0:T(8,128)S(1)}, f32[6,384]{1,0:T(8,128)}, u32[]{:S(2)}) copy-start(f32[6,384]{1,0:T(8,128)} %param.40) | copy-start | bytes 27652
  608.8 222.9 %copy-start.39 = (f32[48,3,384]{2,0,1:T(8,128)S(1)}, f32[48,3,384]{2,0,1:T(8,128)}, u32[]{:S(2)}) copy-start(f32[48,3,384]{2,0,1:T(8,128)} %param.28) | copy-start | bytes 663556
  608.8 224.9 %copy-start.36 = (f32[48,4,384]{2,1,0:T(4,128)S(1)}, f32[48,4,384]{2,1,0:T(4,128)}, u32[]{:S(2)}) copy-start(f32[48,4,384]{2,1,0:T(4,128)} %param.34) | copy-start | bytes 884740
  608.8 224.9 %copy-start.42 = (f32[48,4,384]{2,1,0:T(4,128)S(1)}, f32[48,4,384]{2,1,0:T(4,128)}, u32[]{:S(2)}) copy-start(f32[48,4,384]{2,1,0:T(4,128)} %param.36) | copy-start | bytes 884740
  608.8 224.8 %copy-start.43 = (f32[48,4,384]{2,1,0:T(4,128)S(1)}, f32[48,4,384]{2,1,0:T(4,128)}, u32[]{:S(2)}) copy-start(f32[48,4,384]{2,1,0:T(4,128)} %param.35) | copy-start | bytes 884740
  608.8 226.2 %copy-start.38 = (f32[4,384,48]{1,2,0:T(8,128)S(1)}, f32[4,384,48]{1,2,0:T(8,128)}, u32[]{:S(2)}) copy-start(f32[4,384,48]{1,2,0:T(8,128)} %param.37) | copy-start | bytes 884740
  826.0 11.1 %copy-start.1 = (f32[196,768]{1,0:T(8,128)S(1)}, f32[196,768]{1,0:T(8,128)}, u32[]{:S(2)}) copy-start(f32[196,768]{1,0:T(8,128)} %param.25) | copy-start | bytes 1806340
  (38 other events, 135.1 us)
Sparse Core Ops, SparseCore 0:
  532.0 105.2 reduce-scatter.2
  643.1 135.1 reduce-scatter.4
